TPU v7x, 32 devices: a whole 2x2x4 slice. The times are simulated.
32 devices in a mesh: dom: 8 (over z, x), sub: 4 (over y, core).
Axes of the slice: x: 2, y: 2, z: 4, core: 2. Of those that a mesh axis runs over, the one named last changes fastest.
Arguments:
- positions: float32 [3, 1048576], P(None, ('dom', 'sub')), may hold values from -0.11 to 1.11
- velocities: float32 [3, 1048576], P(None, ('dom', 'sub')), may hold values from -3 to 3
- masses: float32 [1048576], P(('dom', 'sub')), may hold values from 0.003 to 0.012
- accel_prev: float32 [3, 1048576], P(None, ('dom', 'sub')), may hold values from -180 to 180
- active: int32 [1048576], P(('dom', 'sub')), may hold values from 0 to 1, as said below
- bucket_top: int32 [4096], P(('dom', 'sub')), may hold values from 0 to 4095
- near_list: int32 [4096, 4], P(('dom', 'sub')), may hold values from 0 to 511, as said below
- cell_list: int32 [4096, 64], P(('dom', 'sub')), may hold values from 0 to 1023
- top_list: int32 [4096, 32], P(('dom', 'sub')), may hold values from 0 to 4095
- essential: int32 [8, 4, 8, 32], P('dom', 'sub'), may hold values from 0 to 511
- work: int32 [1280], P(('dom', 'sub')), may hold values from 0 to 511, as said below
Outputs:
- vel_out: float32 [3, 1048576], P(None, ('dom', 'sub'))
- pos_out: float32 [3, 1048576], P(None, ('dom', 'sub'))
Inputs may be any that keep to these rules, and one draw needn't show every extreme that they name: near_list[n, 0] is the group-local number of bucket n itself; every entry of row n names a bucket of n's group whose top cell differs from n's by at most one in each of the three top-cell coordinates. A bucket holds an active particle exactly when its group-local number appears in its group's block of work. `work`: entries g * 4 * 40 to (g + 1) * 4 * 40 - 1 are the block of domain group g and name distinct group-local buckets; in every group one device holds 128 of the named buckets.
All inputs are finite; a program needn't handle non-finite values.
Results may differ from a plain program's by a relative error of at most 0.0003.
Values sent between devices are 32-bit elements; how exact they have to be, the bound alone decides.
No kernel may reach another device: no remote copies, remote signals or barrier semaphores. Data moves between devices by JAX's collectives and lax.ppermute only.
A program may use at most 64 MiB of HBM per device.

v0:
```python
import jax
import jax.numpy as jnp
from jax import lax
from jax.sharding import PartitionSpec as P

TOP_SIDE = 16
STEPS = 2
TOP = 4096
time_step = 0.01
soften = 0.0025
mass_floor = 0.5


def top_centres(top_ids):
    cell_side = TOP_SIDE
    first_index = top_ids // (cell_side * cell_side)
    second_index = top_ids // cell_side % cell_side
    third_index = top_ids % cell_side
    stacked = jnp.stack([first_index, second_index, third_index]).astype(jnp.float32)
    return (stacked + 0.5) / cell_side


def bucket_moments(places, weights):
    mass_total = jnp.sum(weights, axis=1)
    centre = jnp.sum(places * weights[None], axis=2) / mass_total[None]
    offsets = places - centre[:, :, None]
    radius_sq = jnp.sum(offsets * offsets, axis=0)

    def diagonal(first_axis):
        return jnp.sum(
            weights * (3.0 * offsets[first_axis] * offsets[first_axis] - radius_sq), axis=1
        )

    def crossed(first_axis, second_axis):
        return 3.0 * jnp.sum(weights * offsets[first_axis] * offsets[second_axis], axis=1)

    quadrupole = jnp.stack(
        [diagonal(0), diagonal(1), diagonal(2), crossed(0, 1), crossed(0, 2), crossed(1, 2)]
    )
    return jnp.concatenate([mass_total[None], centre, quadrupole], axis=0)


def top_raw(places, weights, centres):
    offsets = places - centres[:, :, None]
    weighted = weights[None] * offsets
    row_list = [
        weights,
        weighted[0],
        weighted[1],
        weighted[2],
        weighted[0] * offsets[0],
        weighted[1] * offsets[1],
        weighted[2] * offsets[2],
        weighted[0] * offsets[1],
        weighted[0] * offsets[2],
        weighted[1] * offsets[2],
    ]
    return jnp.stack([jnp.sum(row_values, axis=1) for row_values in row_list])


def top_moments(raw_sums, centres):
    mass_total = raw_sums[0]
    safe_mass = jnp.maximum(mass_total, mass_floor)
    first_sums = raw_sums[1:4]
    centre = centres + first_sums / safe_mass[None]
    cov_xx = raw_sums[4] - first_sums[0] * first_sums[0] / safe_mass
    cov_yy = raw_sums[5] - first_sums[1] * first_sums[1] / safe_mass
    cov_zz = raw_sums[6] - first_sums[2] * first_sums[2] / safe_mass
    cov_xy = raw_sums[7] - first_sums[0] * first_sums[1] / safe_mass
    cov_xz = raw_sums[8] - first_sums[0] * first_sums[2] / safe_mass
    cov_yz = raw_sums[9] - first_sums[1] * first_sums[2] / safe_mass
    trace_sum = cov_xx + cov_yy + cov_zz
    quadrupole = jnp.stack(
        [
            3.0 * cov_xx - trace_sum,
            3.0 * cov_yy - trace_sum,
            3.0 * cov_zz - trace_sum,
            3.0 * cov_xy,
            3.0 * cov_xz,
            3.0 * cov_yz,
        ]
    )
    return jnp.concatenate([mass_total[None], centre, quadrupole], axis=0)


def pair_accel(targets, sources, source_mass):
    offsets = sources[:, :, None] - targets[:, None, :]
    distance = jnp.sum(offsets * offsets, axis=0) + soften
    inverse = lax.rsqrt(distance)
    strength = source_mass[:, None] * inverse * inverse * inverse
    return jnp.sum(offsets * strength[None], axis=1)


def cell_accel(targets, moments):
    offsets = targets[:, None, :] - moments[1:4, :, None]
    distance = jnp.sum(offsets * offsets, axis=0) + soften
    inverse = lax.rsqrt(distance)
    inverse_sq = inverse * inverse
    inverse_three = inverse * inverse_sq
    inverse_five = inverse_three * inverse_sq
    inverse_seven = inverse_five * inverse_sq
    quadrupole = moments[4:10, :, None]
    along_x = quadrupole[0] * offsets[0] + quadrupole[3] * offsets[1] + quadrupole[4] * offsets[2]
    along_y = quadrupole[3] * offsets[0] + quadrupole[1] * offsets[1] + quadrupole[5] * offsets[2]
    along_z = quadrupole[4] * offsets[0] + quadrupole[5] * offsets[1] + quadrupole[2] * offsets[2]
    contracted = offsets[0] * along_x + offsets[1] * along_y + offsets[2] * along_z
    radial = -moments[0][:, None] * inverse_three - 2.5 * contracted * inverse_seven
    along_all = jnp.stack([along_x, along_y, along_z])
    return jnp.sum(offsets * radial[None] + along_all * inverse_five[None], axis=1)


def force_one(
    target, near_ids, cell_ids, top_ids, group_places, group_mass, essential_cells, top_cells
):
    sources = group_places[:, near_ids].reshape(3, -1)
    source_mass = group_mass[near_ids].reshape(-1)
    moments = jnp.concatenate(
        [jnp.take(essential_cells, cell_ids, axis=1), jnp.take(top_cells, top_ids, axis=1)], axis=1
    )
    return pair_accel(target, sources, source_mass) + cell_accel(target, moments)


def in_blocks(step_function, inputs, item_count):
    block_width = 4

    def reshape_leaf(values):
        return values.reshape((item_count // block_width, block_width) + values.shape[1:])

    result = lax.map(jax.vmap(step_function), jax.tree.map(reshape_leaf, inputs))
    return result.reshape((item_count,) + result.shape[2:])


def body(
    positions,
    velocities,
    masses,
    accel_prev,
    active,
    bucket_top,
    near_list,
    cell_list,
    top_list,
    essential,
    work,
):
    bucket_count = bucket_top.shape[0]
    bucket_size = positions.shape[1] // bucket_count
    sub_count = lax.axis_size("sub")
    dom_count = lax.axis_size("dom")
    sub_index = lax.axis_index("sub")
    group_buckets = sub_count * bucket_count
    activity = active.astype(jnp.float32)
    bucket_centres = top_centres(bucket_top)
    all_top_ids = jnp.arange(TOP, dtype=jnp.int32)
    placement = (bucket_top[:, None] == all_top_ids[None, :]).astype(jnp.float32)
    incoming = lax.all_to_all(
        essential.reshape(dom_count, -1), "dom", split_axis=0, concat_axis=0, tiled=True
    ).reshape(-1)
    shared_near, shared_cells, shared_tops, shared_work = (
        lax.all_gather(near_list, "sub", axis=0, tiled=True),
        lax.all_gather(cell_list, "sub", axis=0, tiled=True),
        lax.all_gather(top_list, "sub", axis=0, tiled=True),
        lax.all_gather(work, "sub", axis=0, tiled=True),
    )
    work_near = shared_near[work]
    work_cells = shared_cells[work]
    work_tops = shared_tops[work]
    own_ids = sub_index * bucket_count + jnp.arange(bucket_count, dtype=jnp.int32)
    matches = (own_ids[:, None] == shared_work[None, :]).astype(jnp.float32)
    places = positions
    speeds = velocities
    accel_now = accel_prev
    for substep in range(STEPS):
        half_speed = speeds + 0.5 * time_step * activity * accel_now
        places = places + time_step * half_speed
        group_places, group_mass = (
            lax.all_gather(places, "sub", axis=1, tiled=True),
            lax.all_gather(masses, "sub", axis=0, tiled=True),
        )
        group_places = group_places.reshape(3, group_buckets, bucket_size)
        group_mass = group_mass.reshape(group_buckets, bucket_size)
        group_cells = bucket_moments(group_places, group_mass)
        replies = lax.all_to_all(
            jnp.take(group_cells, incoming, axis=1), "dom", split_axis=1, concat_axis=1, tiled=True
        )
        essential_cells = lax.all_gather(replies, "sub", axis=1, tiled=True)
        own_places = places.reshape(3, bucket_count, bucket_size)
        own_mass = masses.reshape(bucket_count, bucket_size)
        spread_sums = jnp.dot(
            top_raw(own_places, own_mass, bucket_centres),
            placement,
            precision=lax.Precision.HIGHEST,
        )
        totals = lax.psum(spread_sums, ("dom", "sub"))
        top_cells = top_moments(totals, top_centres(all_top_ids))

        def one_bucket(work_item):
            target, near_ids, cell_ids, top_ids = work_item
            return force_one(
                target,
                near_ids,
                cell_ids,
                top_ids,
                group_places,
                group_mass,
                essential_cells,
                top_cells,
            )

        targets = jnp.transpose(group_places[:, work], (1, 0, 2))
        forces = in_blocks(one_bucket, (targets, work_near, work_cells, work_tops), work.shape[0])
        returned = lax.all_gather(forces, "sub", axis=0, tiled=True)
        accel_own = jnp.einsum("bw,wcp->cbp", matches, returned, precision=lax.Precision.HIGHEST)
        accel_now = accel_own.reshape(3, -1)
        speeds = half_speed + 0.5 * time_step * activity * accel_now
    return (speeds, places)


def solution(mesh):
    in_specs = (
        P(None, ("dom", "sub")),
        P(None, ("dom", "sub")),
        P(("dom", "sub")),
        P(None, ("dom", "sub")),
        P(("dom", "sub")),
        P(("dom", "sub")),
        P(("dom", "sub"), None),
        P(("dom", "sub"), None),
        P(("dom", "sub"), None),
        P("dom", "sub", None, None),
        P(("dom", "sub")),
    )
    out_specs = (P(None, ("dom", "sub")), P(None, ("dom", "sub")))
    return jax.shard_map(body, mesh=mesh, in_specs=in_specs, out_specs=out_specs, check_vma=False)
```

profile of v0, /device:TPU:0, one launch (start us, length us, event | category | flops | bytes accessed | tf_op | source)
XLA Modules:
  0.0 734.8 jit_solution(12766479794120827817)
XLA Ops:
  15.1 7.3 all-to-all-start
  22.4 7.3 all_gather.36
  30.0 7.7 %all_gather.37 = s32[512,64]{1,0:T(8,128)S(1)} all-gather(s32[128,64]{1,0:T(8,128)S(1)} %copy.152), channel_id=1, replica_groups=mesh['dom'=8,'sub'=4] {'sub'}, dimensions={0}, use_global_device_ids=true | all-gather | bytes 163840 | tf_op jit(solution)/shard_map/all_gather | solution.py:161
  37.9 6.9 all_gather.39
  45.3 5.8 all_gather.34
  55.8 4.8 all-reduce
  62.0 91.1 %all-reduce.4.cloned.1.call-done = f32[10,4096]{1,0:T(8,128)} async-done(((f32[10,4096]{1,0:T(8,128)}), f32[10,4096]{1,0:T(8,128)}) %all-reduce.4.cloned.1.call-update) | async-done | bytes 163856 | tf_op jit(solution)/shard_map/psum | solution.py:194
  169.5 4.5 all-to-all-start.1
  182.1 5.4 all_gather.38
  188.4 178.6 %while.20 = (s32[]{:T(128)}, f32[10,4,3,256]{3,2,1,0:T(4,128)}, s32[10,4,4]{2,1,0:T(4,128)S(1)}, f32[3,512,256]{2,0,1:T(4,128)S(1)}, f32[10,4,3,256]{3,1,2,0:T(4...) while((s32[]{:T(128)}, f32[10,4,3,256]{3,2,1,0:T(4,128)}, ...), condition=%wide.region_25.29_spmd, body=%wide.region_20.28_spmd.sunk | while | flops 29599920 | bytes 26094408 | solution.py:129
  189.8 4.1 fusion.112
  194.5 2.7 multiply_multiply_fusion.18
  207.7 4.1 fusion.112
  212.4 2.7 multiply_multiply_fusion.18
  225.5 4.1 fusion.112
  230.3 2.7 multiply_multiply_fusion.18
  243.4 4.1 fusion.112
  248.1 2.7 multiply_multiply_fusion.18
  261.2 4.1 fusion.112
  266.0 2.7 multiply_multiply_fusion.18
  279.1 4.1 fusion.112
  283.8 2.7 multiply_multiply_fusion.18
  296.9 4.1 fusion.112
  301.7 2.7 multiply_multiply_fusion.18
  314.8 4.1 fusion.112
  319.5 2.7 multiply_multiply_fusion.18
  332.7 4.1 fusion.112
  337.4 2.7 multiply_multiply_fusion.18
  350.5 4.1 fusion.112
  355.2 2.7 multiply_multiply_fusion.18
  368.0 7.1 all_gather.40
  381.0 129.9 %all-reduce.6.cloned.1.call-done = f32[10,4096]{1,0:T(8,128)} async-done(((f32[10,4096]{1,0:T(8,128)}), f32[10,4096]{1,0:T(8,128)}) %all-reduce.6.cloned.1.call-update) | async-done | bytes 163856 | tf_op jit(solution)/shard_map/psum | solution.py:194
  527.3 4.5 all-to-all-start.2
  535.5 2.9 all-to-all-done.2
  539.3 5.2 all_gather.43
  544.8 172.8 %while.21 = (s32[]{:T(128)}, f32[10,4,3,256]{3,2,1,0:T(4,128)S(1)}, s32[10,4,4]{2,1,0:T(4,128)S(1)}, f32[3,512,256]{2,0,1:T(4,128)S(1)}, f32[10,4,3,256]{3,1,2,0...) while((s32[]{:T(128)}, f32[10,4,3,256]{3,2,1,0:T(4,128)S(1)}, ...), condition=%wide.region_49.53_spmd, body=%wide.region_44.52_spmd.sunk | while | flops 29599920 | bytes 26098504 | solution.py:129
  546.2 4.1 fusion.120
  563.5 4.1 fusion.120
  580.8 4.1 fusion.120
  598.1 4.1 fusion.120
  602.8 2.7 multiply_multiply_fusion.20
  615.3 4.1 fusion.120
  632.6 4.1 fusion.120
  649.9 4.1 fusion.120
  667.2 4.1 fusion.120
  684.5 4.1 fusion.120
  701.7 4.1 fusion.120
  717.7 7.2 all_gather.44
  (812 shorter events, 306.7 us)
Async XLA Ops:
  8.0 145.0 %all-reduce.4.cloned.1.call-start = ((), (), s32[]{:S(2)}) async-start(), calls=%async_computation.4 | async-start | bytes 524288 | tf_op jit(solution)/shard_map/psum | solution.py:194
  9.0 4.0 copy-start.11
  10.8 2.2 copy-start.22
  10.8 2.2 copy-start.16
  10.8 2.2 copy-start.28
  12.4 2.2 copy-start.2
  12.5 10.0 %copy-start.14 = (f32[32768]{0:T(1024)S(1)}, f32[32768]{0:T(1024)}, u32[]{:S(2)}) copy-start(f32[32768]{0:T(1024)} %param.23) | copy-start | bytes 393220
  12.5 17.3 %copy-start.27 = (s32[128,4]{0,1:T(4,128)S(1)}, s32[128,4]{0,1:T(4,128)}, u32[]{:S(2)}) copy-start(s32[128,4]{0,1:T(4,128)} %param.27) | copy-start | bytes 6148
  12.5 17.4 %copy-start.30 = (s32[40]{0:T(128)S(1)}, s32[40]{0:T(128)}, u32[]{:S(2)}) copy-start(s32[40]{0:T(128)} %param.31) | copy-start | bytes 484
  12.5 17.4 %copy-start.15 = (s32[128,64]{0,1:T(8,128)S(1)}, s32[128,64]{0,1:T(8,128)}, u32[]{:S(2)}) copy-start(s32[128,64]{0,1:T(8,128)} %param.28) | copy-start | bytes 98308
  12.5 25.3 %copy-start.18 = (s32[128,32]{0,1:T(8,128)S(1)}, s32[128,32]{0,1:T(8,128)}, u32[]{:S(2)}) copy-start(s32[128,32]{0,1:T(8,128)} %param.29) | copy-start | bytes 49156
  14.6 141.4 %all-gather.3.cloned.1.call-start = ((), (), s32[]{:S(2)}) async-start(), calls=%async_computation.3 | async-start | bytes 2621440 | tf_op jit(solution)/shard_map/all_gather | solution.py:177
  15.1 39.2 %copy-start.31 = (u32[32]{0:T(128)S(1)}, u32[32]{0:T(128)}, u32[]{:S(2)}) copy-start(u32[32]{0:T(128)} %constant.197) | copy-start | bytes 388
  15.1 45.5 %all-to-all-start = ((s32[8,1,32]{2,1,0:T(1,128)}), s32[8,1,32]{2,1,0:T(1,128)S(1)}, u32[]{:S(2)}, u32[]{:S(2)}) async-start(s32[8,1,32]{2,1,0:T(1,128)} %bitcast.56), calls=%async_computation | async-start | bytes 8192 | tf_op jit(solution)/shard_map/all_to_all | solution.py:156
  29.9 147.3 %copy-start.19 = (s32[1024]{0:T(1024)}, s32[1024]{0:T(1024)S(1)}, u32[]{:S(2)}) copy-start(s32[1024]{0:T(1024)S(1)} %pad_clamp_fusion.7) | copy-start | bytes 12292
  61.9 105.9 %copy-start.20 = (s32[1024]{0:T(1024)}, s32[1024]{0:T(1024)S(1)}, u32[]{:S(2)}) copy-start(s32[1024]{0:T(1024)S(1)} %pad_clamp_fusion.6) | copy-start | bytes 12292
  62.0 106.6 %copy-start.25 = (pred[256]{0:T(512)(128)(4,1)}, pred[256]{0:T(512)(128)(4,1)S(1)}, u32[]{:S(2)}) copy-start(pred[256]{0:T(512)(128)(4,1)S(1)} %compare_and_fusion.4) | copy-start | bytes 772
  155.9 2.3 copy-start.1
  169.5 11.1 %all-to-all-start.1 = ((f32[8,1,320]{2,1,0:T(1,128)}), f32[8,1,320]{2,1,0:T(1,128)S(1)}, u32[]{:S(2)}, u32[]{:S(2)}) async-start(f32[8,1,320]{2,1,0:T(1,128)} %reshape.930), calls=%async_computation.1 | async-start | bytes 24576 | tf_op jit(solution)/shard_map/all_to_all | solution.py:183
  174.0 336.9 %all-reduce.6.cloned.1.call-start = ((), (), s32[]{:S(2)}) async-start(), calls=%async_computation.6 | async-start | bytes 524288 | tf_op jit(solution)/shard_map/psum | solution.py:194
  367.0 11.0 %copy-start.3 = (f32[3,32768]{1,0:T(4,128)S(1)}, f32[3,32768]{1,0:T(4,128)}, u32[]{:S(2)}) copy-start(f32[3,32768]{1,0:T(4,128)} %copy-done.2) | copy-start | bytes 1179652
  367.0 11.0 %copy-start.4 = (f32[3,32768]{1,0:T(4,128)S(1)}, f32[3,32768]{1,0:T(4,128)}, u32[]{:S(2)}) copy-start(f32[3,32768]{1,0:T(4,128)} %param.22) | copy-start | bytes 1179652
  367.0 11.0 %copy-start.6 = (f32[3,32768]{1,0:T(4,128)S(1)}, f32[3,32768]{1,0:T(4,128)}, u32[]{:S(2)}) copy-start(f32[3,32768]{1,0:T(4,128)} %param.24) | copy-start | bytes 1179652
  367.0 11.0 %copy-start.12 = (f32[32768]{0:T(1024)S(1)}, f32[32768]{0:T(1024)}, u32[]{:S(2)}) copy-start(f32[32768]{0:T(1024)} %copy-done.11) | copy-start | bytes 393220
  376.7 1.7 copy-start.17
  377.2 0.8 copy-start.9
  378.0 0.8 copy-start.23
  378.0 0.9 copy-start.29
  378.4 2.3 copy-start.8
  380.4 134.3 %all-gather.5.cloned.1.call-start = ((), (), s32[]{:S(2)}) async-start(), calls=%async_computation.5 | async-start | bytes 2621440 | tf_op jit(solution)/shard_map/all_gather | solution.py:177
  514.8 2.2 copy-start
  522.1 4.2 copy-start.26
  527.3 11.1 %all-to-all-start.2 = ((f32[8,1,320]{2,1,0:T(1,128)}), f32[8,1,320]{2,1,0:T(1,128)S(1)}, u32[]{:S(2)}, u32[]{:S(2)}) async-start(f32[8,1,320]{2,1,0:T(1,128)} %reshape.932), calls=%async_computation.2 | async-start | bytes 24576 | tf_op jit(solution)/shard_map/all_to_all | solution.py:183
  544.8 180.1 %copy-start.21 = (s32[160]{0:T(256)S(1)}, s32[160]{0:T(256)}, u32[]{:S(2)}) copy-start(s32[160]{0:T(256)} %all-reduce) | copy-start | bytes 1924
  544.8 180.1 %copy-start.24 = (s32[128]{0:T(128)S(1)}, s32[128]{0:T(128)}, u32[]{:S(2)}) copy-start(s32[128]{0:T(128)} %iota_add_fusion) | copy-start | bytes 1540
  717.6 8.7 %copy-start.5 = (f32[3,32768]{1,0:T(4,128)S(1)}, f32[3,32768]{1,0:T(4,128)}, u32[]{:S(2)}) copy-start(f32[3,32768]{1,0:T(4,128)} %param.22) | copy-start | bytes 1179652
  717.6 8.7 %copy-start.7 = (f32[3,32768]{1,0:T(4,128)S(1)}, f32[3,32768]{1,0:T(4,128)}, u32[]{:S(2)}) copy-start(f32[3,32768]{1,0:T(4,128)} %param.24) | copy-start | bytes 1179652
  717.6 8.7 %copy-start.10 = (f32[1,3,128,256]{3,1,2,0:T(4,128)S(1)}, f32[1,3,128,256]{3,1,2,0:T(4,128)}, u32[]{:S(2)}) copy-start(f32[1,3,128,256]{3,1,2,0:T(4,128)} %copy-done.9) | copy-start | bytes 1179652
  717.6 8.7 %copy-start.13 = (f32[32768]{0:T(1024)S(1)}, f32[32768]{0:T(1024)}, u32[]{:S(2)}) copy-start(f32[32768]{0:T(1024)} %copy-done.11) | copy-start | bytes 393220
Sparse Core Ops, SparseCore 0:
  14.9 138.1 all-reduce.3
  380.5 130.3 all-reduce.5
Sparse Core Ops, SparseCore 1:
  17.2 27.6 all-gather.2
  383.0 21.0 all-gather.4
where the time goes:
time: 738 us; the launch traced here: 735 us
  other arithmetic  275 us (37%)
  waiting for transfers between devices  227 us (31%)
  local copies, waits for them, and re-layouts  135 us (18%)
  blocking collectives  57.5 us (8%)
  between operations  16.9 us (2%)
  starting transfers between devices  16.8 us (2%)
    psum x2, waiting for transfers between devices, body(): totals = lax.psum(spread_sums, ('dom', 'sub'))  221 us
    reduce_sum x20, other arithmetic, pair_accel(): distance = jnp.sum(offsets * offsets, axis=0) + soften  82.5 us
    mul x20, other arithmetic, pair_accel(): strength = source_mass[:, None] * inverse * inverse * inverse  53.3 us
    gather x40, local copies, waits for them, and re-layouts, force_one(): jnp.take(top_cells, top_ids, axis=1)  46.6 us
    reduce_sum x20, other arithmetic, pair_accel(): return jnp.sum(offsets * strength[None], axis=1)  39.3 us
    gather x40, local copies, waits for them, and re-layouts, force_one(): jnp.take(essential_cells, cell_ids, axis=1)  16.5 us
  transfers between devices with their start and end apart: 7, of which 4 were waited for; matrix products, arithmetic and copies ran while one was open for 3% of the time, Pallas kernels for 0%

commit v1 on v0

--- a/solution.py
+++ b/solution.py
@@ -191,7 +191,7 @@
             placement,
             precision=lax.Precision.HIGHEST,
         )
-        totals = lax.psum(spread_sums, ("dom", "sub"))
+        totals = jnp.sum(lax.all_gather(spread_sums, ("dom", "sub")), axis=0)
         top_cells = top_moments(totals, top_centres(all_top_ids))
 
         def one_bucket(work_item):

time: 738 us -> 626 us (0.85)
  waiting for transfers between devices: 227 us -> 97.7 us
  other arithmetic: 275 us -> 285 us
    psum x2 -> x0, waiting for transfers between devices: 221 us -> none  [body(): totals = lax.psum(spread_sums, ('dom', 'sub'))]
    all_gather x0 -> x2, waiting for transfers between devices: none -> 74.6 us  [body(): totals = jnp.sum(lax.all_gather(spread_sums, ('dom', 'sub')), axis=0)]
    all_gather x2, waiting for transfers between devices: 0.05 us -> 18 us  [body(): lax.all_gather(places, 'sub', axis=1, tiled=True)]
    reduce_sum x0 -> x2, other arithmetic: none -> 8.53 us  [body(): totals = jnp.sum(lax.all_gather(spread_sums, ('dom', 'sub')), axis=0)]
  transfers between devices with their start and end apart: 7 -> 7, of which waited for: 4 -> 4; matrix products, arithmetic and copies ran while one was open for 3% -> 7% of each run, Pallas kernels for 0% -> 0%
where the time goes in v1:
time: 626 us; the launch traced here: 623 us
  other arithmetic  285 us (46%)
  local copies, waits for them, and re-layouts  138 us (22%)
  waiting for transfers between devices  97.7 us (16%)
  blocking collectives  61 us (10%)
  starting transfers between devices  18.7 us (3%)
  between operations  15.2 us (2%)
    reduce_sum x20, other arithmetic, pair_accel(): distance = jnp.sum(offsets * offsets, axis=0) + soften  82.5 us
    all_gather x2, waiting for transfers between devices, body(): totals = jnp.sum(lax.all_gather(spread_sums, ('dom', 'sub')), axis=0)  74.6 us
    mul x20, other arithmetic, pair_accel(): strength = source_mass[:, None] * inverse * inverse * inverse  53.3 us
    gather x40, local copies, waits for them, and re-layouts, force_one(): jnp.take(top_cells, top_ids, axis=1)  46.6 us
    reduce_sum x20, other arithmetic, pair_accel(): return jnp.sum(offsets * strength[None], axis=1)  39.3 us
    all_gather x2, waiting for transfers between devices, body(): lax.all_gather(places, 'sub', axis=1, tiled=True)  18 us
    gather x40, local copies, waits for them, and re-layouts, force_one(): jnp.take(essential_cells, cell_ids, axis=1)  16.4 us
    sub x40, local copies, waits for them, and re-layouts, pair_accel(): offsets = sources[:, :, None] - targets[:, None, :]  14.4 us
  transfers between devices with their start and end apart: 7, of which 4 were waited for; matrix products, arithmetic and copies ran while one was open for 7% of the time, Pallas kernels for 0%

profile of v1, /device:TPU:0, one launch (start us, length us, event | category | flops | bytes accessed | tf_op | source)
XLA Modules:
  0.0 622.6 jit_solution(13951072991283799642)
XLA Ops:
  14.1 7.3 %all-to-all-start = ((s32[8,1,32]{2,1,0:T(1,128)}), s32[8,1,32]{2,1,0:T(1,128)S(1)}, u32[]{:S(2)}, u32[]{:S(2)}) async-start(s32[8,1,32]{2,1,0:T(1,128)} %bitcast.56), calls=%async_computation | async-start | bytes 8192 | tf_op jit(solution)/shard_map/all_to_all | solution.py:156
  21.6 7.7 %all_gather.49 = s32[512,64]{1,0:T(8,128)S(1)} all-gather(s32[128,64]{1,0:T(8,128)S(1)} %copy.148), channel_id=1, replica_groups=mesh['dom'=8,'sub'=4] {'sub'}, dimensions={0}, use_global_device_ids=true | all-gather | bytes 163840 | tf_op jit(solution)/shard_map/all_gather | solution.py:161
  29.8 9.9 %all_gather.48 = f32[131072]{0:T(1024)S(1)} all-gather(f32[32768]{0:T(1024)S(1)} %copy-done.12), channel_id=1, replica_groups=mesh['dom'=8,'sub'=4] {'sub'}, dimensions={0}, use_global_device_ids=true | all-gather | bytes 655360 | tf_op jit(solution)/shard_map/all_gather | solution.py:178
  40.3 5.8 all_gather.46
  63.7 5.5 all-to-all-start.1
  69.3 7.6 %all_gather.51 = s32[512,32]{1,0:T(8,128)S(1)} all-gather(s32[128,32]{1,0:T(8,128)} %copy.156), channel_id=1, replica_groups=mesh['dom'=8,'sub'=4] {'sub'}, dimensions={0}, use_global_device_ids=true | all-gather | bytes 81920 | tf_op jit(solution)/shard_map/all_gather | solution.py:162
  80.4 4.8 all-reduce
  88.1 5.6 all_gather.50
  93.9 26.0 %all-gather.13.cloned.1.call-done = f32[32,10,4096]{2,1,0:T(8,128)} async-done(((f32[1,10,4096]{2,1,0:T(8,128)}), f32[32,10,4096]{2,1,0:T(8,128)}) %all-gather.13.cloned.1.call-update) | async-done | bytes 5242896 | tf_op jit(solution)/shard_map/all_gather | solution.py:194
  119.9 4.6 reduce_sum.446
  129.9 2.9 copy.159
  133.5 171.9 %while.20 = (s32[]{:T(128)}, f32[10,4,3,256]{3,2,1,0:T(4,128)}, s32[10,4,4]{2,1,0:T(4,128)S(1)}, f32[3,512,256]{2,0,1:T(4,128)S(1)}, f32[10,4,3,256]{3,1,2,0:T(4...) while((s32[]{:T(128)}, f32[10,4,3,256]{3,2,1,0:T(4,128)}, ...), condition=%wide.region_25.29_spmd, body=%wide.region_20.28_spmd.sunk | while | flops 29599920 | bytes 26094908 | solution.py:129
  140.7 4.1 fusion.110
  145.5 2.7 multiply_multiply_fusion.18
  157.9 4.1 fusion.110
  162.6 2.7 multiply_multiply_fusion.18
  175.1 4.1 fusion.110
  192.3 4.1 fusion.110
  209.4 4.1 fusion.110
  214.2 2.7 multiply_multiply_fusion.18
  226.7 4.1 fusion.110
  243.8 4.1 fusion.110
  248.5 2.7 multiply_multiply_fusion.18
  261.0 4.1 fusion.110
  278.2 4.1 fusion.110
  283.0 2.7 multiply_multiply_fusion.18
  295.4 4.1 fusion.110
  306.5 7.0 %all_gather.54 = f32[160,3,256]{2,0,1:T(8,128)S(1)} all-gather(f32[40,3,256]{2,0,1:T(8,128)S(1)} %copy.172), channel_id=1, replica_groups=mesh['dom'=8,'sub'=4] {'sub'}, dimensions={0}, use_global_device_ids=true | all-gather | bytes 614400 | tf_op jit(solution)/shard_map/all_gather | solution.py:212
  321.2 18.0 %all-gather.11.cloned.1.call-done = f32[3,131072]{1,0:T(4,128)} async-done(((f32[3,32768]{1,0:T(4,128)}), f32[3,131072]{1,0:T(4,128)}) %all-gather.11.cloned.1.call-update) | async-done | bytes 1572880 | tf_op jit(solution)/shard_map/all_gather | solution.py:177
  351.7 5.5 all-to-all-start.2
  358.7 5.1 all-to-all-done.2
  364.7 5.5 all_gather.57
  370.4 48.6 %all-gather.15.cloned.1.call-done = f32[32,10,4096]{2,1,0:T(8,128)} async-done(((f32[1,10,4096]{2,1,0:T(8,128)}), f32[32,10,4096]{2,1,0:T(8,128)}) %all-gather.15.cloned.1.call-update) | async-done | bytes 5242896 | tf_op jit(solution)/shard_map/all_gather | solution.py:194
  419.0 3.9 reduce_sum.465
  427.4 179.0 %while.21 = (s32[]{:T(128)}, f32[10,4,3,256]{3,2,1,0:T(4,128)S(1)}, s32[10,4,4]{2,1,0:T(4,128)}, f32[3,512,256]{2,0,1:T(4,128)S(1)}, f32[10,4,3,256]{3,1,2,0:T(4...) while((s32[]{:T(128)}, f32[10,4,3,256]{3,2,1,0:T(4,128)S(1)}, ...), condition=%wide.region_49.53_spmd, body=%wide.region_44.52_spmd.sunk | while | flops 29599920 | bytes 26098496 | solution.py:129
  436.0 4.1 fusion.118
  453.8 4.1 fusion.118
  458.6 2.7 multiply_multiply_fusion.20
  471.8 4.1 fusion.118
  476.5 2.7 multiply_multiply_fusion.20
  489.6 4.1 fusion.118
  507.5 4.1 fusion.118
  525.4 4.1 fusion.118
  543.2 4.1 fusion.118
  561.2 4.1 fusion.118
  579.2 4.1 fusion.118
  597.0 4.1 fusion.118
  606.5 7.1 %all_gather.60 = f32[160,3,256]{2,0,1:T(8,128)S(1)} all-gather(f32[40,3,256]{2,0,1:T(8,128)S(1)} %copy.173), channel_id=1, replica_groups=mesh['dom'=8,'sub'=4] {'sub'}, dimensions={0}, use_global_device_ids=true | all-gather | bytes 614400 | tf_op jit(solution)/shard_map/all_gather | solution.py:212
  (830 shorter events, 315.8 us)
Async XLA Ops:
  7.2 3.6 copy-start.12
  7.2 3.7 copy-start.37
  7.2 44.7 %all-gather.9.cloned.1.call-start = ((), (), s32[]{:S(2)}) async-start(), calls=%async_computation.3 | async-start | bytes 2621440 | tf_op jit(solution)/shard_map/all_gather | solution.py:177
  8.2 4.0 copy-start.9
  10.6 10.7 %copy-start.36 = (s32[128,4]{0,1:T(4,128)S(1)}, s32[128,4]{0,1:T(4,128)}, u32[]{:S(2)}) copy-start(s32[128,4]{0,1:T(4,128)} %param.27) | copy-start | bytes 6148
  10.6 10.8 %copy-start.24 = (s32[128,64]{0,1:T(8,128)S(1)}, s32[128,64]{0,1:T(8,128)}, u32[]{:S(2)}) copy-start(s32[128,64]{0,1:T(8,128)} %param.28) | copy-start | bytes 98308
  10.7 19.1 %copy-start.39 = (s32[40]{0:T(128)S(1)}, s32[40]{0:T(128)}, u32[]{:S(2)}) copy-start(s32[40]{0:T(128)} %param.31) | copy-start | bytes 484
  10.7 109.2 %all-gather.13.cloned.1.call-start = ((), (), s32[]{:S(2)}) async-start(), calls=%async_computation.5 | async-start | bytes 8650752 | tf_op jit(solution)/shard_map/all_gather | solution.py:194
  10.9 10.4 %copy-start.31 = (f32[128]{0:T(128)}, f32[128]{0:T(128)S(1)}, u32[]{:S(2)}) copy-start(f32[128]{0:T(128)S(1)} %reduce_sum.436) | copy-start | bytes 1540
  11.0 10.4 %copy-start.25 = (f32[3,128]{1,0:T(4,128)}, f32[3,128]{1,0:T(4,128)S(1)}, u32[]{:S(2)}) copy-start(f32[3,128]{1,0:T(4,128)S(1)} %fusion.84) | copy-start | bytes 4612
  12.4 36.2 %copy-start.27 = (s32[128,32]{0,1:T(8,128)S(1)}, s32[128,32]{0,1:T(8,128)}, u32[]{:S(2)}) copy-start(s32[128,32]{0,1:T(8,128)} %param.29) | copy-start | bytes 49156
  14.1 35.5 %all-to-all-start = ((s32[8,1,32]{2,1,0:T(1,128)}), s32[8,1,32]{2,1,0:T(1,128)S(1)}, u32[]{:S(2)}, u32[]{:S(2)}) async-start(s32[8,1,32]{2,1,0:T(1,128)} %bitcast.56), calls=%async_computation | async-start | bytes 8192 | tf_op jit(solution)/shard_map/all_to_all | solution.py:156
  29.8 24.2 %copy-start.28 = (s32[1024]{0:T(1024)}, s32[1024]{0:T(1024)S(1)}, u32[]{:S(2)}) copy-start(s32[1024]{0:T(1024)S(1)} %pad_clamp_fusion.7) | copy-start | bytes 12292
  49.5 4.5 copy-start.21
  51.9 2.9 copy-start.1
  54.0 0.8 copy-start.19
  60.4 0.8 copy-start.20
  60.4 0.8 copy-start.22
  63.7 22.9 %all-to-all-start.1 = ((f32[8,1,320]{2,1,0:T(1,128)}), f32[8,1,320]{2,1,0:T(1,128)S(1)}, u32[]{:S(2)}, u32[]{:S(2)}) async-start(f32[8,1,320]{2,1,0:T(1,128)} %reshape.938), calls=%async_computation.1 | async-start | bytes 24576 | tf_op jit(solution)/shard_map/all_to_all | solution.py:183
  69.2 269.9 %all-gather.11.cloned.1.call-start = ((), (), s32[]{:S(2)}) async-start(), calls=%async_computation.4 | async-start | bytes 2621440 | tf_op jit(solution)/shard_map/all_gather | solution.py:177
  93.9 33.5 %copy-start.13 = (s32[1,4096]{1,0:T(1,128)S(1)}, s32[1,4096]{1,0:T(1,128)}, u32[]{:S(2)}) copy-start(s32[1,4096]{1,0:T(1,128)} %get-tuple-element.336) | copy-start | bytes 49156
  93.9 33.5 %copy-start.15 = (s32[1,4096]{1,0:T(1,128)S(1)}, s32[1,4096]{1,0:T(1,128)}, u32[]{:S(2)}) copy-start(s32[1,4096]{1,0:T(1,128)} %get-tuple-element.337) | copy-start | bytes 49156
  124.5 9.0 %copy-start.17 = (s32[40,4]{1,0:T(8,128)S(1)}, s32[40,4]{1,0:T(8,128)}, u32[]{:S(2)}) copy-start(s32[40,4]{1,0:T(8,128)} %gather_fusion.8) | copy-start | bytes 1924
  133.5 180.0 %copy-start.29 = (s32[160]{0:T(256)S(1)}, s32[160]{0:T(256)}, u32[]{:S(2)}) copy-start(s32[160]{0:T(256)} %all-reduce) | copy-start | bytes 1924
  133.5 180.0 %copy-start.33 = (s32[128]{0:T(128)S(1)}, s32[128]{0:T(128)}, u32[]{:S(2)}) copy-start(s32[128]{0:T(128)} %iota_add_fusion) | copy-start | bytes 1540
  305.4 12.4 %copy-start.18 = (s32[10,4,32]{2,1,0:T(4,128)}, s32[10,4,32]{2,1,0:T(4,128)S(1)}, u32[]{:S(2)}) copy-start(s32[10,4,32]{2,1,0:T(4,128)S(1)} %get-tuple-element.606) | copy-start | bytes 15364
  305.4 11.2 %copy-start.2 = (f32[3,32768]{1,0:T(4,128)S(1)}, f32[3,32768]{1,0:T(4,128)}, u32[]{:S(2)}) copy-start(f32[3,32768]{1,0:T(4,128)} %multiply_add_fusion.2) | copy-start | bytes 1179652
  305.4 11.2 %copy-start.3 = (f32[3,32768]{1,0:T(4,128)S(1)}, f32[3,32768]{1,0:T(4,128)}, u32[]{:S(2)}) copy-start(f32[3,32768]{1,0:T(4,128)} %param.22) | copy-start | bytes 1179652
  305.4 11.2 %copy-start.5 = (f32[3,32768]{1,0:T(4,128)S(1)}, f32[3,32768]{1,0:T(4,128)}, u32[]{:S(2)}) copy-start(f32[3,32768]{1,0:T(4,128)} %param.24) | copy-start | bytes 1179652
  305.4 11.2 %copy-start.10 = (f32[32768]{0:T(1024)S(1)}, f32[32768]{0:T(1024)}, u32[]{:S(2)}) copy-start(f32[32768]{0:T(1024)} %copy-done.9) | copy-start | bytes 393220
  316.3 1.8 copy-start.26
  316.6 2.7 copy-start.7
  316.6 2.9 copy-start.32
  316.7 3.0 copy-start.38
  317.8 101.2 %all-gather.15.cloned.1.call-start = ((), (), s32[]{:S(2)}) async-start(), calls=%async_computation.6 | async-start | bytes 8650752 | tf_op jit(solution)/shard_map/all_gather | solution.py:194
  319.3 22.0 %copy-start.23 = (f32[512]{0:T(512)S(1)}, f32[512]{0:T(512)}, u32[]{:S(2)}) copy-start(f32[512]{0:T(512)} %copy-done.21) | copy-start | bytes 6148
  339.1 2.2 copy-start
  346.6 4.2 copy-start.35
  351.7 12.1 %all-to-all-start.2 = ((f32[8,1,320]{2,1,0:T(1,128)}), f32[8,1,320]{2,1,0:T(1,128)S(1)}, u32[]{:S(2)}, u32[]{:S(2)}) async-start(f32[8,1,320]{2,1,0:T(1,128)} %reshape.940), calls=%async_computation.2 | async-start | bytes 24576 | tf_op jit(solution)/shard_map/all_to_all | solution.py:183
  370.4 53.9 %copy-start.14 = (s32[1,4096]{1,0:T(1,128)S(1)}, s32[1,4096]{1,0:T(1,128)}, u32[]{:S(2)}) copy-start(s32[1,4096]{1,0:T(1,128)} %get-tuple-element.336) | copy-start | bytes 49156
  370.4 53.9 %copy-start.16 = (s32[1,4096]{1,0:T(1,128)S(1)}, s32[1,4096]{1,0:T(1,128)}, u32[]{:S(2)}) copy-start(s32[1,4096]{1,0:T(1,128)} %get-tuple-element.337) | copy-start | bytes 49156
  427.4 186.2 %copy-start.30 = (s32[160]{0:T(256)S(1)}, s32[160]{0:T(256)}, u32[]{:S(2)}) copy-start(s32[160]{0:T(256)} %all-reduce) | copy-start | bytes 1924
  427.4 186.2 %copy-start.34 = (s32[128]{0:T(128)S(1)}, s32[128]{0:T(128)}, u32[]{:S(2)}) copy-start(s32[128]{0:T(128)} %iota_add_fusion) | copy-start | bytes 1540
  606.4 8.6 %copy-start.4 = (f32[3,32768]{1,0:T(4,128)S(1)}, f32[3,32768]{1,0:T(4,128)}, u32[]{:S(2)}) copy-start(f32[3,32768]{1,0:T(4,128)} %param.22) | copy-start | bytes 1179652
  606.4 8.6 %copy-start.6 = (f32[3,32768]{1,0:T(4,128)S(1)}, f32[3,32768]{1,0:T(4,128)}, u32[]{:S(2)}) copy-start(f32[3,32768]{1,0:T(4,128)} %param.24) | copy-start | bytes 1179652
  606.4 8.6 %copy-start.8 = (f32[1,3,128,256]{3,1,2,0:T(4,128)S(1)}, f32[1,3,128,256]{3,1,2,0:T(4,128)}, u32[]{:S(2)}) copy-start(f32[1,3,128,256]{3,1,2,0:T(4,128)} %copy-done.7) | copy-start | bytes 1179652
  606.4 8.6 %copy-start.11 = (f32[32768]{0:T(1024)S(1)}, f32[32768]{0:T(1024)}, u32[]{:S(2)}) copy-start(f32[32768]{0:T(1024)} %copy-done.9) | copy-start | bytes 393220
Sparse Core Ops, SparseCore 0:
  10.8 29.3 all-gather.8
  43.0 76.8 all-gather.12
  317.9 21.1 all-gather.10
  341.9 77.0 all-gather.14
